TPU v7x, 256 devices: a whole 4x4x8 slice. The times are simulated.
256 devices in a mesh: dp: 32 (over z, x), tensor: 8 (over y, core).
Axes of the slice: x: 4, y: 4, z: 8, core: 2. Of those that a mesh axis runs over, the one named last changes fastest.
Arguments:
- tokens: bfloat16 [65536, 8192], P('dp', 'tensor'), may hold values from -6 to 6
- base_value_weight: bfloat16 [8192, 1024], P('tensor'), may hold values from -0.0625 to 0.0625
- adapter_down_weight: bfloat16 [512, 8192, 64], P('dp', 'tensor'), may hold values from -0.0625 to 0.0625
- adapter_up_weight: bfloat16 [512, 64, 1024], P('dp', None, 'tensor'), may hold values from -0.75 to 0.75
- request_adapter_index: int32 [128], P('dp'), may hold values from 0 to 511
- storage_index_table: int32 [512], replicated, may hold values from 0 to 511, each once
Outputs:
- values_out: bfloat16 [65536, 1024], P('dp', 'tensor')
Inputs may be any that keep to these rules, and one draw needn't show every extreme that they name: `request_adapter_index`: each adapter id names an adapter. storage_index_table is a permutation of the storage positions.
All inputs are finite; a program needn't handle non-finite values.
Results may differ from a plain program's by a relative error of at most 0.003.
Values may be sent and summed in bfloat16 or wider, within the bound.
A program may use at most 128 MiB of HBM per device.

v0:
```python
import jax
import jax.numpy as jnp
from jax import lax
from jax.sharding import PartitionSpec as P

adapter_scale = 0.5


def shards(
    tokens,
    base_value_weight,
    adapter_down_weight,
    adapter_up_weight,
    request_adapter_index,
    storage_index_table,
):
    n_rows, width = tokens.shape
    requests_here = request_adapter_index.shape[0]
    seq_len = n_rows // requests_here
    owned_columns = adapter_down_weight.shape[0]
    adapter_rank_size = adapter_down_weight.shape[2]
    local_columns = adapter_up_weight.shape[2]
    all_adapters = storage_index_table.shape[0]
    down_width = width * adapter_rank_size
    base_projection = lax.psum_scatter(
        lax.dot_general(
            base_value_weight, tokens, (((0,), (1,)), ((), ())), preferred_element_type=jnp.float32
        ),
        "tensor",
        scatter_dimension=0,
        tiled=True,
    ).T
    every_id = lax.all_gather(request_adapter_index, "dp", axis=0, tiled=True)
    catalog = lax.broadcasted_iota(jnp.int32, (every_id.shape[0], all_adapters), 1)
    picked = (every_id[:, None] == catalog).astype(jnp.int32)
    positions = jnp.sum(picked * storage_index_table[None, :], axis=1)
    local_place = positions - lax.axis_index("dp") * owned_columns
    owner_slots = lax.broadcasted_iota(jnp.int32, (every_id.shape[0], owned_columns), 1)
    match = (local_place[:, None] == owner_slots).astype(jnp.bfloat16)
    panels = jnp.concatenate(
        (
            adapter_down_weight.reshape(owned_columns, down_width),
            adapter_up_weight.reshape(owned_columns, adapter_rank_size * local_columns),
        ),
        axis=1,
    )
    outgoing = jnp.dot(match, panels, preferred_element_type=jnp.bfloat16)
    outgoing = outgoing.reshape(lax.axis_size("dp"), requests_here, panels.shape[1])
    fetched = jnp.sum(
        lax.all_to_all(outgoing, "dp", split_axis=0, concat_axis=0, tiled=True), axis=0
    )
    down_sel = fetched[:, :down_width].reshape(requests_here, width, adapter_rank_size)
    up_sel = fetched[:, down_width:].reshape(requests_here, adapter_rank_size, local_columns)
    grouped = tokens.reshape(requests_here, seq_len, width)
    low_part = jnp.einsum("rsd,rdk->rsk", grouped, down_sel, preferred_element_type=jnp.float32)
    low = lax.psum(low_part, "tensor").astype(jnp.bfloat16)
    adapter_update = jnp.einsum("rsk,rkc->rsc", low, up_sel, preferred_element_type=jnp.float32)
    adapter_update = adapter_update.reshape(n_rows, local_columns)
    return (base_projection + adapter_scale * adapter_update).astype(jnp.bfloat16)


def solution(mesh):
    return jax.shard_map(
        shards,
        mesh=mesh,
        in_specs=(
            P("dp", "tensor"),
            P("tensor", None),
            P("dp", "tensor", None),
            P("dp", None, "tensor"),
            P("dp"),
            P(),
        ),
        out_specs=P("dp", "tensor"),
        check_vma=False,
    )
```

profile of v0, /device:TPU:102, one launch (start us, length us, event | category | flops | bytes accessed | tf_op | source)
XLA Modules:
  0.0 573.9 jit_solution(4957867999160425157)
XLA Ops:
  6.5 0.0 copy-start
  6.5 1.4 dynamic-slice
  8.6 0.9 dynamic-update-slice
  9.5 19.0 %all-reduce = s32[128]{0:T(128)S(1)} all-reduce(s32[128]{0:T(128)S(1)} %dynamic-update-slice), channel_id=1, replica_groups=mesh['dp'=32,'tensor'=8] {'dp'}, use_global_device_ids=true, to_apply=%add | all-reduce | flops 128 | bytes 1024
  28.5 4.8 copy.12
  33.3 0.0 copy-start.2
  33.3 0.0 copy-start.3
  33.3 5.8 %reshape.26 = bf16[16,65536]{1,0:T(8,128)(2,1)} reshape(bf16[16,1024,64]{2,1,0:T(8,128)(2,1)} %copy.12) | data formatting | bytes 4194304 | tf_op jit(solution)/shard_map/reshape | solution.py:42
  39.0 0.0 copy-done.2
  39.0 0.2 copy.25
  39.2 0.0 copy-done.3
  39.2 0.2 select_reduce_fusion
  39.4 10.7 %fusion = bf16[128,73728]{1,0:T(8,128)(2,1)} fusion(bf16[16,8192]{1,0:T(8,128)(2,1)S(1)} %bitcast.25, bf16[16,65536]{1,0:T(8,128)(2,1)} %reshape.26, s32[128]{0:T(128)S(1)} %broadcast_subtract_fusion), kind=kOutput, calls=%fused_computation | convolution fusion | flops 306710528 | bytes 21234176 | tf_op jit(solution)/shard_map/dot_general | solution.py:47
  50.1 21.1 %reshape.28 = bf16[32,4,73728]{2,1,0:T(4,128)(2,1)} reshape(bf16[128,73728]{1,0:T(8,128)(2,1)} %fusion) | data formatting | bytes 37748736 | tf_op jit(solution)/shard_map/reshape | solution.py:48
  71.2 8.3 %all-to-all-start = ((bf16[32,4,73728]{2,1,0:T(4,128)(2,1)}), bf16[32,4,73728]{2,1,0:T(4,128)(2,1)}, u32[]{:S(2)}, u32[]{:S(2)}) async-start(bf16[32,4,73728]{2,1,0:T(4,128)(2,1)} %reshape.28), calls=%async_computation.1 | async-start | bytes 37748736 | tf_op jit(solution)/shard_map/all_to_all | solution.py:50
  79.5 0.0 reduce-scatter.2.cloned.1.call-start
  79.6 0.0 copy-done
  79.6 8.9 %fusion.10 = f32[1024,2048]{1,0:T(8,128)} fusion(bf16[1024,1024]{1,0:T(8,128)(2,1)S(1)} %copy-done, bf16[2048,1024]{1,0:T(8,128)(2,1)} %param.6), kind=kOutput, calls=%fused_computation.19 | convolution fusion | flops 4294967296 | bytes 14680064 | tf_op jit(solution)/shard_map/dot_general | solution.py:26
  88.5 0.0 reduce-scatter.2.cloned.1.call-update
  88.6 423.3 %all-to-all-done = bf16[32,4,73728]{2,1,0:T(4,128)(2,1)} async-done(((bf16[32,4,73728]{2,1,0:T(4,128)(2,1)}), bf16[32,4,73728]{2,1,0:T(4,128)(2,1)}, u32[]{:S(2)}, u32[]{:S(2)}) %all-to-all-start) | async-done | bytes 18874400 | tf_op jit(solution)/shard_map/all_to_all | solution.py:50
  511.9 9.3 %reduce_sum.22 = bf16[4,73728]{1,0:T(4,128)(2,1)S(1)} reduce(bf16[32,4,73728]{2,1,0:T(4,128)(2,1)} %all-to-all-done, bf16[]{:T(256)} %constant.14.clone.1), dimensions={0}, to_apply=%region_2.0 | reduce | flops 9142272 | bytes 19464194 | tf_op jit(solution)/shard_map/reduce_sum | solution.py:49
  521.2 0.0 copy-start.1
  521.2 0.8 copy-done.1
  522.0 1.0 slice.8
  523.0 1.9 reshape.29
  524.9 4.4 convolution_bitcast_fusion
  529.3 0.9 slice_bitcast_fusion
  530.2 29.8 %all-reduce.2 = bf16[4,512,64]{1,2,0:T(8,128)(2,1)S(1)} all-reduce(f32[4,512,64]{1,2,0:T(8,128)} %convolution_bitcast_fusion), channel_id=1, replica_groups=mesh['dp'=32,'tensor'=8] {'tensor'}, use_global_device_ids=true, to_apply=%region_3.0 | all-reduce | flops 131072 | bytes 786432 | tf_op jit(solution)/shard_map/psum | solution.py:56
  560.0 1.3 convolution_multiply_fusion
  561.3 1.6 copy.17
  562.9 0.0 reduce-scatter.2.cloned.1.call-done
  562.9 2.1 fusion.4
  565.0 2.0 copy.15
  (2 shorter events, 0.0 us)
Async XLA Ops:
  6.5 73.1 %copy-start = (bf16[1024,1024]{1,0:T(8,128)(2,1)S(1)}, bf16[1024,1024]{1,0:T(8,128)(2,1)}, u32[]{:S(2)}) copy-start(bf16[1024,1024]{1,0:T(8,128)(2,1)} %param.7) | copy-start | bytes 6291460
  33.3 5.8 %copy-start.2 = (bf16[16,64,128]{2,1,0:T(8,128)(2,1)S(1)}, bf16[16,64,128]{2,1,0:T(8,128)(2,1)}, u32[]{:S(2)}) copy-start(bf16[16,64,128]{2,1,0:T(8,128)(2,1)} %param.9) | copy-start | bytes 786436
  33.3 5.9 %copy-start.3 = (s32[512]{0:T(512)S(1)}, s32[512]{0:T(512)}, u32[]{:S(2)}) copy-start(s32[512]{0:T(512)} %param.11) | copy-start | bytes 6148
  71.2 440.7 %all-to-all-start = ((bf16[32,4,73728]{2,1,0:T(4,128)(2,1)}), bf16[32,4,73728]{2,1,0:T(4,128)(2,1)}, u32[]{:S(2)}, u32[]{:S(2)}) async-start(bf16[32,4,73728]{2,1,0:T(4,128)(2,1)} %reshape.28), calls=%async_computation.1 | async-start | bytes 37748736 | tf_op jit(solution)/shard_map/all_to_all | solution.py:50
  79.5 483.3 %reduce-scatter.2.cloned.1.call-start = ((), (), s32[]{:S(2)}) async-start(), calls=%async_computation.2 | async-start | bytes 9437184 | tf_op jit(solution)/shard_map/reduce_scatter | solution.py:25
  521.2 0.8 copy-start.1
Sparse Core Ops, SparseCore 0:
  88.7 56.3 reduce-scatter.1
where the time goes:
time: 575 us; the launch traced here: 574 us
  waiting for transfers between devices  423 us (74%)
  blocking collectives  48.8 us (8%)
  local copies, waits for them, and re-layouts  42.2 us (7%)
  matrix products  25.4 us (4%)
  between operations  14.2 us (2%)
  other arithmetic  11.6 us (2%)
  starting transfers between devices  8.39 us (1%)
    all_to_all x1, waiting for transfers between devices, shards(): lax.all_to_all(outgoing, 'dp', split_axis=0, concat_axis=0, tiled=True)  423 us
    psum x1, blocking collectives, shards(): low = lax.psum(low_part, 'tensor').astype(jnp.bfloat16)  29.8 us
    reshape x1, local copies, waits for them, and re-layouts, shards(): outgoing.reshape(lax.axis_size('dp'), requests_here, panels.shape[1])  21.1 us
    unnamed x1, blocking collectives  19 us
  transfers between devices with their start and end apart: 2, of which 1 were waited for; matrix products, arithmetic and copies ran while one was open for 5% of the time, Pallas kernels for 0%

commit v1 on v0

v1 whole, which is shorter than its diff:
```python
import jax
import jax.numpy as jnp
from jax import lax
from jax.sharding import PartitionSpec as P

adapter_scale = 0.5


def shards(
    tokens,
    base_value_weight,
    adapter_down_weight,
    adapter_up_weight,
    request_adapter_index,
    storage_index_table,
):
    n_rows, width = tokens.shape
    requests_here = request_adapter_index.shape[0]
    seq_len = n_rows // requests_here
    owned = adapter_down_weight.shape[0]
    rank = adapter_down_weight.shape[2]
    local_columns = adapter_up_weight.shape[2]
    n_dp = lax.axis_size("dp")

    down_t = jnp.swapaxes(adapter_down_weight, 1, 2)
    pieces = jnp.concatenate(
        (
            down_t.reshape(owned, n_dp, rank * width // n_dp // 128, 128),
            adapter_up_weight.reshape(owned, n_dp, rank * local_columns // n_dp // 128, 128),
        ),
        axis=2,
    )
    pieces = jnp.swapaxes(pieces, 0, 1)
    held = lax.all_to_all(pieces, "dp", split_axis=0, concat_axis=0, tiled=True)
    held = held.reshape(n_dp * owned, -1, 128)

    every_id = lax.all_gather(request_adapter_index, "dp", axis=0, tiled=True)
    positions = storage_index_table[every_id]
    outgoing = held[positions].reshape(n_dp, requests_here, -1, 128)
    fetched = lax.all_to_all(outgoing, "dp", split_axis=0, concat_axis=0, tiled=True)
    fetched = jnp.swapaxes(fetched, 0, 1)
    down_rows = rank * width // n_dp // 128
    down_sel = fetched[:, :, :down_rows].reshape(requests_here, rank, width)
    up_sel = fetched[:, :, down_rows:].reshape(requests_here, rank, local_columns)

    base_projection = lax.psum_scatter(
        lax.dot_general(
            base_value_weight, tokens, (((0,), (1,)), ((), ())), preferred_element_type=jnp.float32
        ),
        "tensor",
        scatter_dimension=0,
        tiled=True,
    ).T

    grouped = tokens.reshape(requests_here, seq_len, width)
    low_part = jnp.einsum("rsd,rkd->rks", grouped, down_sel, preferred_element_type=jnp.float32)
    low = lax.psum(low_part, "tensor").astype(jnp.bfloat16)
    adapter_update = jnp.einsum("rks,rkc->rsc", low, up_sel, preferred_element_type=jnp.float32)
    adapter_update = adapter_update.reshape(n_rows, local_columns)
    return (base_projection + adapter_scale * adapter_update).astype(jnp.bfloat16)


def solution(mesh):
    return jax.shard_map(
        shards,
        mesh=mesh,
        in_specs=(
            P("dp", "tensor"),
            P("tensor", None),
            P("dp", "tensor", None),
            P("dp", None, "tensor"),
            P("dp"),
            P(),
        ),
        out_specs=P("dp", "tensor"),
        check_vma=False,
    )
```

time: 575 us -> 182 us (0.32)
  the two profiles are of different devices: /device:TPU:102 before, /device:TPU:1 now
where the time goes in v1:
time: 182 us; the launch traced here: 180 us
  blocking collectives  110 us (60%)
  local copies, waits for them, and re-layouts  24.9 us (14%)
  between operations  14.2 us (8%)
  matrix products  13.9 us (8%)
  starting transfers between devices  12.1 us (7%)
  other arithmetic  4.53 us (2%)
    unnamed x1, blocking collectives  56.1 us
    psum x1, blocking collectives, shards(): low = lax.psum(low_part, 'tensor').astype(jnp.bfloat16)  30.3 us
    all_to_all x1, blocking collectives, shards(): lax.all_to_all(outgoing, 'dp', split_axis=0, concat_axis=0, tiled=True)  23.5 us
    all_to_all x1, starting transfers between devices, shards(): held = lax.all_to_all(pieces, 'dp', split_axis=0, concat_axis=0, tiled=True)  12.1 us
    dot_general x1, matrix products, shards(): lax.dot_general(base_value_weight, tokens, (((0,), (1,)), ((), ())), pref...  8.96 us
    reshape x1, local copies, waits for them, and re-layouts, shards(): down_t.reshape(owned, n_dp, rank * width // n_dp // 128, 128)  4.24 us
    transpose x1, local copies, waits for them, and re-layouts, shards(): pieces = jnp.swapaxes(pieces, 0, 1)  4.18 us
  transfers between devices with their start and end apart: 2, of which 0 were waited for; matrix products, arithmetic and copies ran while one was open for 16% of the time, Pallas kernels for 0%

profile of v1, /device:TPU:1, one launch (start us, length us, event | category | flops | bytes accessed | tf_op | source)
XLA Modules:
  0.0 179.6 jit_solution(14180586535549913768)
XLA Ops:
  6.5 0.0 copy-start
  6.5 0.0 reduce-scatter.2.cloned.1.call-start
  6.5 1.6 copy-done
  8.1 9.0 %fusion.3 = f32[1024,2048]{1,0:T(8,128)} fusion(bf16[1024,1024]{1,0:T(8,128)(2,1)S(1)} %copy-done, bf16[2048,1024]{1,0:T(8,128)(2,1)} %param.6), kind=kOutput, calls=%fused_computation.12 | convolution fusion | flops 4294967296 | bytes 14680064 | tf_op jit(solution)/shard_map/dot_general | solution.py:47
  17.1 0.0 reduce-scatter.2.cloned.1.call-update
  17.1 0.0 copy-start.2
  17.1 4.2 %reshape.37 = bf16[16,32,16,128]{3,2,1,0:T(8,128)(2,1)} reshape(bf16[16,64,1024]{2,1,0:T(8,128)(2,1)} %bitcast.33) | data formatting | bytes 4194304 | tf_op jit(solution)/shard_map/reshape | solution.py:28
  21.4 0.0 copy-done.2
  21.4 2.4 %maximum_bitcast_fusion = bf16[32,16,18,128]{3,2,0,1:T(8,128)(2,1)S(1)} fusion(bf16[16,32,2,128]{3,2,1,0:T(2,128)(2,1)S(1)} %bitcast.35, bf16[16,32,16,128]{3,2,1,0:T(8,128)(2,1)} %reshape.37), kind=kLoop, calls=%fused_computation.2 | loop fusion | flops 4718592 | bytes 4718592 | tf_op jit(solution)/shard_map/transpose | solution.py:33
  23.8 4.2 %copy.23 = bf16[32,16,18,128]{3,1,2,0:T(8,128)(2,1)} copy(bf16[32,16,18,128]{3,2,0,1:T(8,128)(2,1)S(1)} %maximum_bitcast_fusion) | data formatting | bytes 4718592 | tf_op jit(solution)/shard_map/transpose | solution.py:33
  27.9 0.0 copy-start.4
  28.0 0.0 copy-start.3
  28.0 0.0 copy-start.1
  28.0 12.1 %all-to-all-start = ((bf16[32,16,18,128]{3,1,2,0:T(8,128)(2,1)}), bf16[32,16,18,128]{3,1,2,0:T(8,128)(2,1)}, u32[]{:S(2)}, u32[]{:S(2)}) async-start(bf16[32,16,18,128]{3,1,2,0:T(8,128)(2,1)} %copy.23), calls=%async_computation.1 | async-start | bytes 4718592 | tf_op jit(solution)/shard_map/all_to_all | solution.py:34
  40.1 0.0 copy-done.4
  40.1 0.6 dynamic-slice
  41.3 0.0 copy-done.3
  41.3 0.2 dynamic-update-slice
  41.6 56.1 %all-reduce = s32[128]{0:T(128)S(1)} all-reduce(s32[128]{0:T(128)S(1)} %dynamic-update-slice), channel_id=1, replica_groups=mesh['dp'=32,'tensor'=8] {'dp'}, use_global_device_ids=true, to_apply=%add | all-reduce | flops 128 | bytes 1024
  97.7 0.0 copy-done.1
  97.7 1.3 gather_fusion
  99.0 0.0 all-to-all-done
  99.0 2.3 %copy.24 = bf16[32,16,18,128]{3,1,0,2:T(8,128)(2,1)S(1)} copy(bf16[32,16,18,128]{3,1,2,0:T(8,128)(2,1)} %all-to-all-done) | data formatting | bytes 4718592 | tf_op jit(solution)/shard_map/all_to_all | solution.py:34
  101.3 3.4 %copy.25 = bf16[512,18,128]{2,1,0:T(8,128)(2,1)} copy(bf16[512,18,128]{2,0,1:T(8,128)(2,1)S(1)} %bitcast.27) | data formatting | bytes 4718592 | tf_op jit(solution)/shard_map/reshape | solution.py:35
  104.7 2.6 %gather_fusion.1 = bf16[128,18,128]{2,1,0:T(8,128)(2,1)S(1)} fusion(bf16[512,18,128]{2,1,0:T(8,128)(2,1)} %copy.25, s32[1024]{0:T(1024)S(1)} %pad_clamp_fusion), kind=kCustom, calls=%fused_computation.1 | custom fusion | bytes 1180160 | tf_op jit(solution)/shard_map/gather | solution.py:39
  107.3 0.2 copy.27
  107.6 23.5 %all_to_all.10 = bf16[32,4,18,128]{3,1,2,0:T(4,128)(2,1)S(1)} all-to-all(bf16[32,4,18,128]{3,1,2,0:T(4,128)(2,1)S(1)} %copy.27), channel_id=1, replica_groups=mesh['dp'=32,'tensor'=8] {'dp'}, dimensions={0} | all-to-all | bytes 1179648 | tf_op jit(solution)/shard_map/all_to_all | solution.py:40
  131.1 0.3 slice.12
  131.4 0.1 copy.28
  131.5 0.2 reshape.41
  131.7 3.6 %fusion.4 = f32[4,64,512]{2,1,0:T(8,128)S(1)} fusion(bf16[4,64,1024]{2,1,0:T(8,128)(2,1)S(1)} %reshape.41, bf16[4,512,1024]{2,1,0:T(8,128)(2,1)} %bitcast.28), kind=kOutput, calls=%fused_computation.13 | convolution fusion | flops 268435456 | bytes 5242880 | tf_op jit(solution)/shard_map/rsd,rkd->rks/dot_general | solution.py:56
  135.3 0.1 copy.29
  135.3 30.3 %all-reduce.2 = bf16[4,64,512]{2,1,0:T(8,128)(2,1)S(1)} all-reduce(f32[4,64,512]{2,1,0:T(8,128)S(1)} %fusion.4), channel_id=1, replica_groups=mesh['dp'=32,'tensor'=8] {'tensor'}, use_global_device_ids=true, to_apply=%region_1.0 | all-reduce | flops 131072 | bytes 786432 | tf_op jit(solution)/shard_map/psum | solution.py:57
  165.6 1.4 convolution_multiply_fusion
  167.0 1.6 copy.35
  168.6 0.0 reduce-scatter.2.cloned.1.call-done
  168.6 2.1 %fusion = bf16[2048,128]{0,1:T(8,128)(2,1)} fusion(f32[2048,128]{0,1:T(8,128)S(1)} %copy.35, f32[128,2048]{1,0:T(8,128)} %reduce-scatter.2.cloned.1.call-done), kind=kLoop, calls=%fused_computation.5 | loop fusion | flops 524288 | bytes 2621440 | tf_op jit(solution)/shard_map/convert_element_type | solution.py:60
  170.8 2.0 %copy.31 = bf16[2048,128]{1,0:T(8,128)(2,1)} copy(bf16[2048,128]{0,1:T(8,128)(2,1)} %fusion) | data formatting | bytes 1048576 | tf_op jit(solution)/shard_map/convert_element_type | solution.py:60
  (6 shorter events, 0.1 us)
Async XLA Ops:
  6.5 1.6 copy-start
  6.5 162.1 %reduce-scatter.2.cloned.1.call-start = ((), (), s32[]{:S(2)}) async-start(), calls=%async_computation.3 | async-start | bytes 9437184 | tf_op jit(solution)/shard_map/reduce_scatter | solution.py:46
  17.1 4.3 %copy-start.2 = (bf16[16,64,128]{2,1,0:T(8,128)(2,1)S(1)}, bf16[16,64,128]{2,1,0:T(8,128)(2,1)}, u32[]{:S(2)}) copy-start(bf16[16,64,128]{2,1,0:T(8,128)(2,1)} %param.9) | copy-start | bytes 786436
  27.9 12.1 %copy-start.4 = (u32[256]{0:T(256)S(1)}, u32[256]{0:T(256)}, u32[]{:S(2)}) copy-start(u32[256]{0:T(256)} %constant.11) | copy-start | bytes 3076
  28.0 13.4 %copy-start.3 = (s32[4]{0:T(128)S(1)}, s32[4]{0:T(128)}, u32[]{:S(2)}) copy-start(s32[4]{0:T(128)} %param.10) | copy-start | bytes 52
  28.0 69.8 %copy-start.1 = (s32[512]{0:T(512)S(1)}, s32[512]{0:T(512)}, u32[]{:S(2)}) copy-start(s32[512]{0:T(512)} %param.11) | copy-start | bytes 6148
  28.0 71.1 %all-to-all-start = ((bf16[32,16,18,128]{3,1,2,0:T(8,128)(2,1)}), bf16[32,16,18,128]{3,1,2,0:T(8,128)(2,1)}, u32[]{:S(2)}, u32[]{:S(2)}) async-start(bf16[32,16,18,128]{3,1,2,0:T(8,128)(2,1)} %copy.23), calls=%async_computation.1 | async-start | bytes 4718592 | tf_op jit(solution)/shard_map/all_to_all | solution.py:34
Sparse Core Ops, SparseCore 0:
  17.2 58.2 reduce-scatter.1

commit v2 on v1

v2 whole, which is shorter than its diff:
```python
import functools

import jax
import jax.numpy as jnp
from jax import lax
from jax.experimental import pallas as pl
from jax.experimental.pallas import tpu as pltpu
from jax.sharding import PartitionSpec as P

MESH = pl.DeviceIdType.MESH
adapter_scale = 0.5
LANES = 128
ROWS = 16
SLOTS = 4
VMEM_LIMIT = 60 * 1024 * 1024


def iota(shape, axis):
    return lax.broadcasted_iota(jnp.int32, shape, axis)


def visit(q, n):
    half = q // 2 + 1
    return half + (q % 2) * (n - 2 * half)


def ids_kernel(n_dp, owned, upr, ids_ref, table_ref, row_ref, col_ref, mine, every, send_sem, recv_sem):
    dp = lax.axis_index("dp")
    shift = owned.bit_length() - 1
    rp = SLOTS * upr
    slot = iota((rp, LANES), 0) // upr
    tile = jnp.zeros((rp, LANES), jnp.int32)
    for s in range(SLOTS):
        tile = jnp.where(slot == s, ids_ref[s], tile)
    mine[...] = tile
    every[dp] = tile

    barrier = pltpu.get_barrier_semaphore()

    def greet(q, _):
        peer = lax.rem(dp + q, n_dp)
        pl.semaphore_signal(barrier, inc=1, device_id={"dp": peer}, device_id_type=MESH)
        return 0

    lax.fori_loop(1, n_dp, greet, 0)
    pl.semaphore_wait(barrier, n_dp - 1)

    def push(step):
        return pltpu.make_async_remote_copy(
            src_ref=mine,
            dst_ref=every.at[dp],
            send_sem=send_sem.at[step],
            recv_sem=recv_sem.at[step],
            device_id={"dp": lax.rem(dp + step, n_dp)},
            device_id_type=MESH,
        )

    def go(step, _):
        push(step).start()
        return 0

    def come(step, _):
        push(step).wait()
        return 0

    lax.fori_loop(1, n_dp, go, 0)
    lax.fori_loop(1, n_dp, come, 0)

    n = n_dp * rp
    ids = every[...].reshape(n, LANES)
    blocks = table_ref.shape[1] // LANES
    lane = iota((n, LANES), 1)
    pos = jnp.zeros((n, 1), jnp.int32)
    for b in range(blocks):
        row = table_ref[:, b * LANES : (b + 1) * LANES]
        hit = ids == lane + b * LANES
        pos += jnp.sum(jnp.where(hit, row, 0), axis=1, keepdims=True)
    owner = lax.shift_right_logical(pos, shift)
    rank = jnp.zeros((n, 1), jnp.int32)
    count = jnp.zeros((n, 1), jnp.int32)
    for b in range(blocks):
        at = lane + b * LANES
        needed = jnp.max(jnp.where(pos == at, 1, 0), axis=0, keepdims=True)
        same = jnp.where(lax.shift_right_logical(at, shift) == owner, needed, 0)
        count += jnp.sum(same, axis=1, keepdims=True)
        rank += jnp.sum(jnp.where(at < pos, same, 0), axis=1, keepdims=True)
    code = owner * owned + rank
    col_ref[...] = jnp.broadcast_to(code, (n, LANES))
    for b in range(n // LANES):
        diag = iota((n, LANES), 0) == lane + b * LANES
        row_ref[0:1, b * LANES : (b + 1) * LANES] = jnp.sum(jnp.where(diag, code, 0), axis=0, keepdims=True)
    own = jnp.where((owner == dp) & (rank == lane), pos - dp * owned, 0)
    row_ref[1:2, 0:LANES] = jnp.max(own, axis=0, keepdims=True)
    row_ref[2:3, 0:LANES] = jnp.broadcast_to(jnp.max(count, axis=0, keepdims=True), (1, LANES))


def main_kernel(
    n_dp, n_t, k, upr,
    row_ref, col_ref, tok_hbm, w_hbm, down_hbm, up_hbm, out_ref,
    tok, w, down, up, upt, stage, held, outb, land, part, pair, anti, fwd, bwd, hop_a, hop_b, got_f, got_b,
    panel, lowp, lowr, lowb, lowa,
    load_sem, s1, r1, s2, r2, sp, rp_, sh, rh, s3, r3, s4, r4,
):
    dp = lax.axis_index("dp")
    t = lax.axis_index("tensor")
    y, c = t // 2, t % 2
    n_y = n_t // 2
    n_rows, width = tok.shape
    owned, rank, _ = down.shape
    seq = n_rows // SLOTS
    ncg = width // LANES
    nu = -(-upr * k // ROWS)
    nt = k + nu
    nuo = -(-SLOTS * upr // ROWS)
    no = SLOTS + nuo
    rp = SLOTS * upr
    half = n_rows // 2
    tb = n_rows // n_t

    loads = [
        pltpu.make_async_copy(a, b, load_sem.at[i])
        for i, (a, b) in enumerate(((down_hbm, down), (up_hbm, up), (tok_hbm, tok), (w_hbm, w)))
    ]
    for cp in loads:
        cp.start()

    barrier = pltpu.get_barrier_semaphore()

    def greet_dp(q, _):
        pl.semaphore_signal(barrier, inc=1, device_id={"dp": lax.rem(dp + q, n_dp)}, device_id_type=MESH)
        return 0

    def greet_t(q, _):
        pl.semaphore_signal(barrier, inc=1, device_id={"tensor": lax.rem(t + q, n_t)}, device_id_type=MESH)
        return 0

    lax.fori_loop(1, n_dp, greet_dp, 0)
    lax.fori_loop(1, n_t, greet_t, 0)

    loads[0].wait()
    loads[1].wait()

    def pick(j, _):
        which = row_ref[1, j]
        for i in range(n_dp):
            rg, cg = divmod(i, ncg)
            stage[i * nt + j] = down[which, rg * ROWS : (rg + 1) * ROWS, cg * LANES : (cg + 1) * LANES]
        return 0

    lax.fori_loop(0, k, pick, 0)
    kk = nu * ROWS // upr
    for j in range(kk):
        upt[j * rank : (j + 1) * rank, :] = up[row_ref[1, min(j, k - 1)]]
    m = n_dp * nu * ROWS
    r = iota((m, kk * rank), 0)
    src = (r % (nu * ROWS)) // upr * rank + r // (nu * ROWS) * upr + r % upr
    perm = jnp.where(src == iota((m, kk * rank), 1), 1.0, 0.0).astype(jnp.bfloat16)
    ups = jnp.dot(perm, upt[0 : kk * rank, :], preferred_element_type=jnp.float32).astype(jnp.bfloat16)
    for i in range(n_dp):
        for u in range(nu):
            b = i * nu + u
            stage[i * nt + k + u] = ups[b * ROWS : (b + 1) * ROWS, :]

    pl.semaphore_wait(barrier, n_dp - 1 + n_t - 1)

    def exchange(src_ref, dst_ref, size, send_sem, recv_sem, step):
        peer = lax.rem(dp + step, n_dp)
        return pltpu.make_async_remote_copy(
            src_ref=src_ref.at[pl.ds(peer * size, size)],
            dst_ref=dst_ref.at[pl.ds(dp * size, size)],
            send_sem=send_sem.at[step],
            recv_sem=recv_sem.at[step],
            device_id={"dp": peer},
            device_id_type=MESH,
        )

    def start_all(make):
        def body(q, _):
            make(visit(q, n_dp)).start()
            return 0

        lax.fori_loop(0, n_dp - 1, body, 0)

    def wait_all(make, kind):
        def body(q, _):
            cp = make(visit(q, n_dp))
            cp.wait_recv() if kind == "recv" else cp.wait_send()
            return 0

        lax.fori_loop(0, n_dp - 1, body, 0)

    first = functools.partial(exchange, stage, held, nt, s1, r1)
    second = functools.partial(exchange, outb, land, no, s2, r2)

    start_all(first)

    def keep1(b, _):
        held[dp * nt + b] = stage[dp * nt + b]
        return 0

    lax.fori_loop(0, nt, keep1, 0)

    loads[2].wait()
    loads[3].wait()

    def to_tensor(src_ref, dst_ref, send_sem, recv_sem, peer):
        return pltpu.make_async_remote_copy(
            src_ref=src_ref, dst_ref=dst_ref, send_sem=send_sem, recv_sem=recv_sem,
            device_id={"tensor": peer}, device_id_type=MESH,
        )

    partner = t + 1 - 2 * c
    own_cols = pl.ds(pl.multiple_of(c * LANES, LANES), LANES)
    other_cols = pl.ds(pl.multiple_of((1 - c) * LANES, LANES), LANES)
    mb = 256
    pairs = {}
    for rel in (2, 1, 3, 0):
        target = lax.rem(y + rel, n_y)
        cols = pl.ds(pl.multiple_of(target * 2 * LANES, 2 * LANES), 2 * LANES)

        def block(i, _, rel=rel, cols=cols):
            rows = pl.ds(pl.multiple_of(i * mb, mb), mb)
            part[rel, rows, :] = jnp.dot(tok[rows, :], w[:, cols], preferred_element_type=jnp.float32)
            return 0

        lax.fori_loop(0, n_rows // mb, block, 0)
        pairs[rel] = to_tensor(part.at[rel, :, other_cols], pair.at[rel], sp.at[rel], rp_.at[rel], partner)
        pairs[rel].start()

    ahead = lax.rem(y + 1, n_y) * 2 + c
    behind = lax.rem(y + n_y - 1, n_y) * 2 + c
    lo, hi = pl.ds(0, half), pl.ds(half, half)

    def both(rel, rows):
        return part[rel, rows, own_cols] + pair[rel, rows, :]

    send_a = to_tensor(anti.at[lo], hop_a, sh.at[0], rh.at[0], ahead)
    send_b = to_tensor(anti.at[hi], hop_b, sh.at[1], rh.at[1], behind)
    fwd_hi = to_tensor(fwd.at[hi], got_f.at[hi], sh.at[2], rh.at[2], ahead)
    bwd_lo = to_tensor(bwd.at[lo], got_b.at[lo], sh.at[3], rh.at[3], behind)
    fwd_lo = to_tensor(fwd.at[lo], got_f.at[lo], sh.at[4], rh.at[4], ahead)
    bwd_hi = to_tensor(bwd.at[hi], got_b.at[hi], sh.at[5], rh.at[5], behind)

    pairs[2].wait_recv()
    anti[...] = both(2, slice(None)).astype(jnp.bfloat16)
    send_a.start()
    send_b.start()
    pairs[1].wait_recv()
    fwd[hi, :] = both(1, hi).astype(jnp.bfloat16)
    fwd_hi.start()
    pairs[3].wait_recv()
    bwd[lo, :] = both(3, lo).astype(jnp.bfloat16)
    bwd_lo.start()
    send_a.wait_recv()
    fwd[lo, :] = (both(1, lo) + hop_a[...].astype(jnp.float32)).astype(jnp.bfloat16)
    fwd_lo.start()
    send_b.wait_recv()
    bwd[hi, :] = (both(3, hi) + hop_b[...].astype(jnp.float32)).astype(jnp.bfloat16)
    bwd_hi.start()

    wait_all(first, "recv")

    def serve(d, _):
        for s in range(SLOTS):
            code = row_ref[0, d * rp + s * upr]
            outb[d * no + s] = held[lax.div(code, owned) * nt + lax.rem(code, owned)]
        return 0

    lax.fori_loop(0, n_dp, serve, 0)
    source = jnp.concatenate([held[o * nt + k + u] for o in range(n_dp) for u in range(nu)], axis=0)
    shape = (n_dp * rp, n_dp * nu * ROWS)
    code = col_ref[:, 0:1]
    shift = owned.bit_length() - 1
    src = lax.shift_right_logical(code, shift) * (nu * ROWS) + (code & (owned - 1)) * upr
    src = src + iota((n_dp * rp, 1), 0) % upr
    pickup = jnp.where(src == iota(shape, 1), 1.0, 0.0).astype(jnp.bfloat16)
    ups = jnp.dot(pickup, source, preferred_element_type=jnp.float32).reshape(n_dp, rp, LANES)
    if rp < nuo * ROWS:
        ups = jnp.concatenate([ups, jnp.zeros((n_dp, nuo * ROWS - rp, LANES), jnp.float32)], axis=1)
    ups = ups.astype(jnp.bfloat16)
    for d in range(n_dp):
        for u in range(nuo):
            outb[d * no + SLOTS + u] = ups[d, u * ROWS : (u + 1) * ROWS, :]
    start_all(second)

    def keep2(b, _):
        land[dp * no + b] = outb[dp * no + b]
        return 0

    lax.fori_loop(0, no, keep2, 0)
    wait_all(second, "recv")

    for i in range(n_dp):
        rg, cg = divmod(i, ncg)
        for s in range(SLOTS):
            panel[s, rg * ROWS : (rg + 1) * ROWS, cg * LANES : (cg + 1) * LANES] = land[i * no + s]

    per = n_t // SLOTS
    for s in range(SLOTS):
        low = lax.dot_general(
            panel[s], tok[s * seq : (s + 1) * seq, :], (((1,), (1,)), ((), ())),
            preferred_element_type=jnp.float32,
        )
        for h in range(per):
            lowp[s * per + h] = low[:, h * tb : (h + 1) * tb]

    def spread(src, dst, send_sem, recv_sem, step, by_peer):
        peer = lax.rem(t + step, n_t)
        return to_tensor(
            src.at[peer] if by_peer else src, dst.at[t], send_sem.at[step], recv_sem.at[step], peer
        )

    scatter = [spread(lowp, lowr, s3, r3, q, True) for q in range(1, n_t)]
    for cp in scatter:
        cp.start()
    lowr[t] = lowp[t]
    source = jnp.concatenate([land[i * no + SLOTS + u] for i in range(n_dp) for u in range(nuo)], axis=0)
    shape = (SLOTS * rank, n_dp * nuo * ROWS)
    r = iota(shape, 0)
    src = (r % rank) // upr * (nuo * ROWS) + r // rank * upr + r % upr
    perm = jnp.where(src == iota(shape, 1), 1.0, 0.0).astype(jnp.bfloat16)
    ups = jnp.dot(perm, source, preferred_element_type=jnp.float32).astype(jnp.bfloat16)
    for cp in scatter:
        cp.wait_recv()
    total = lowr[0]
    for q in range(1, n_t):
        total = total + lowr[q]
    lowb[...] = total.astype(jnp.bfloat16)
    gather = [spread(lowb, lowa, s4, r4, q, False) for q in range(1, n_t)]
    for cp in gather:
        cp.start()
    lowa[t] = total.astype(jnp.bfloat16)

    pairs[0].wait_recv()
    fwd_hi.wait_recv()
    bwd_lo.wait_recv()
    fwd_lo.wait_recv()
    bwd_hi.wait_recv()
    for cp in gather:
        cp.wait_recv()
    for b in range(n_t):
        rows = pl.ds(b * tb, tb)
        delta = lax.dot_general(
            lowa[b], ups[b // per * rank : (b // per + 1) * rank, :], (((0,), (0,)), ((), ())),
            preferred_element_type=jnp.float32,
        )
        base = both(0, rows) + got_f[rows, :].astype(jnp.float32) + got_b[rows, :].astype(jnp.float32)
        out_ref[rows, :] = (base + adapter_scale * delta).astype(jnp.bfloat16)

    wait_all(first, "send")
    wait_all(second, "send")
    for rel in range(4):
        pairs[rel].wait_send()
    for cp in (send_a, send_b, fwd_hi, bwd_lo, fwd_lo, bwd_hi, *scatter, *gather):
        cp.wait_send()


def gather_ids(n_dp, owned, upr, ids, table):
    n = n_dp * SLOTS * upr
    return pl.pallas_call(
        functools.partial(ids_kernel, n_dp, owned, upr),
        name="gather_ids",
        out_shape=(
            jax.ShapeDtypeStruct((8, n), jnp.int32),
            jax.ShapeDtypeStruct((n, LANES), jnp.int32),
        ),
        in_specs=[pl.BlockSpec(memory_space=pltpu.SMEM), pl.BlockSpec(memory_space=pltpu.VMEM)],
        out_specs=(pl.BlockSpec(memory_space=pltpu.VMEM), pl.BlockSpec(memory_space=pltpu.VMEM)),
        scratch_shapes=[
            pltpu.VMEM((SLOTS * upr, LANES), jnp.int32),
            pltpu.VMEM((n_dp, SLOTS * upr, LANES), jnp.int32),
            pltpu.SemaphoreType.DMA((n_dp,)),
            pltpu.SemaphoreType.DMA((n_dp,)),
        ],
        compiler_params=pltpu.CompilerParams(collective_id=0, has_side_effects=True),
    )(ids, table)


def project(n_dp, n_t, k, upr, collective_id, rows_info, cols_info, tokens, weight, down_t, up):
    n_rows, width = tokens.shape
    owned, rank, columns = up.shape
    nt = k + -(-upr * k // ROWS)
    nuo = -(-SLOTS * upr // ROWS)
    no = SLOTS + nuo
    kk = -(-upr * k // ROWS) * ROWS // upr
    bf, f32 = jnp.bfloat16, jnp.float32
    dma = pltpu.SemaphoreType.DMA
    half, tb = n_rows // 2, n_rows // n_t
    anywhere = pl.BlockSpec(memory_space=pl.ANY)
    return pl.pallas_call(
        functools.partial(main_kernel, n_dp, n_t, k, upr),
        name=f"project_{k}",
        out_shape=jax.ShapeDtypeStruct((n_rows, columns), bf),
        in_specs=[
            pl.BlockSpec(memory_space=pltpu.SMEM),
            pl.BlockSpec(memory_space=pltpu.VMEM),
            anywhere, anywhere, anywhere, anywhere,
        ],
        out_specs=pl.BlockSpec(memory_space=pltpu.VMEM),
        scratch_shapes=[
            pltpu.VMEM((n_rows, width), bf),
            pltpu.VMEM(weight.shape, bf),
            pltpu.VMEM(down_t.shape, bf),
            pltpu.VMEM(up.shape, bf),
            pltpu.VMEM((kk * rank, LANES), bf),
            pltpu.VMEM((n_dp * nt, ROWS, LANES), bf),
            pltpu.VMEM((n_dp * nt, ROWS, LANES), bf),
            pltpu.VMEM((n_dp * no, ROWS, LANES), bf),
            pltpu.VMEM((n_dp * no, ROWS, LANES), bf),
            pltpu.VMEM((4, n_rows, 2 * LANES), f32),
            pltpu.VMEM((4, n_rows, LANES), f32),
            pltpu.VMEM((n_rows, LANES), bf),
            pltpu.VMEM((n_rows, LANES), bf),
            pltpu.VMEM((n_rows, LANES), bf),
            pltpu.VMEM((half, LANES), bf),
            pltpu.VMEM((half, LANES), bf),
            pltpu.VMEM((n_rows, LANES), bf),
            pltpu.VMEM((n_rows, LANES), bf),
            pltpu.VMEM((SLOTS, rank, width), bf),
            pltpu.VMEM((n_t, rank, tb), f32),
            pltpu.VMEM((n_t, rank, tb), f32),
            pltpu.VMEM((rank, tb), bf),
            pltpu.VMEM((n_t, rank, tb), bf),
            dma((4,)),
            dma((n_dp,)), dma((n_dp,)),
            dma((n_dp,)), dma((n_dp,)),
            dma((4,)), dma((4,)),
            dma((6,)), dma((6,)),
            dma((n_t,)), dma((n_t,)),
            dma((n_t,)), dma((n_t,)),
        ],
        compiler_params=pltpu.CompilerParams(
            collective_id=collective_id, has_side_effects=True, vmem_limit_bytes=VMEM_LIMIT
        ),
    )(rows_info, cols_info, tokens, weight, down_t, up)


FEW = 6


def shards(
    tokens,
    base_value_weight,
    adapter_down_weight,
    adapter_up_weight,
    request_adapter_index,
    storage_index_table,
):
    n_dp, n_t = lax.axis_size("dp"), lax.axis_size("tensor")
    owned, width, rank = adapter_down_weight.shape
    upr = rank // n_dp
    down_t = jnp.swapaxes(adapter_down_weight, 1, 2)
    rows_info, cols_info = gather_ids(
        n_dp, owned, upr, request_adapter_index, storage_index_table.reshape(1, -1)
    )
    operands = (rows_info, cols_info, tokens, base_value_weight, down_t, adapter_up_weight)
    return lax.cond(
        rows_info[2, 0] <= FEW,
        functools.partial(project, n_dp, n_t, FEW, upr, 1),
        functools.partial(project, n_dp, n_t, owned, upr, 2),
        *operands,
    )


def solution(mesh):
    return jax.shard_map(
        shards,
        mesh=mesh,
        in_specs=(
            P("dp", "tensor"),
            P("tensor", None),
            P("dp", "tensor", None),
            P("dp", None, "tensor"),
            P("dp"),
            P(),
        ),
        out_specs=P("dp", "tensor"),
        check_vma=False,
    )
```

time: 182 us -> 83.7 us (0.46); the launches traced: 180 us -> 83.6 us
  blocking collectives: 110 us -> 0 us
  Pallas kernels: 0 us -> 81.6 us
  local copies, waits for them, and re-layouts: 24.9 us -> 1.31 us
  matrix products: 13.9 us -> 0 us
  between operations: 14.2 us -> 0.67 us
  starting transfers between devices: 12.1 us -> 0 us
  other arithmetic: 4.53 us -> 0 us
    pallas_call x0 -> x2, Pallas kernels: none -> 81.6 us  [the longest x1 64.7 us: project(): pl.pallas_call(functools.partial(main_kernel, n_dp, n_t, k, upr), name=f'...]
    unnamed x1 -> x0, blocking collectives: 56.1 us -> none
    psum x1 -> x0, blocking collectives: 30.3 us -> none  [shards(): low = lax.psum(low_part, 'tensor').astype(jnp.bfloat16)]
    all_to_all x1 -> x0, blocking collectives: 23.5 us -> none  [shards(): lax.all_to_all(outgoing, 'dp', split_axis=0, concat_axis=0, tiled=True)]
    dot_general x3 -> x0, matrix products: 13.9 us -> none  [the longest x1 8.96 us: shards(): lax.dot_general(base_value_weight, tokens, (((0,), (1,)), ((), ())), pref...]
    all_to_all x1 -> x0, starting transfers between devices: 12.1 us -> none  [shards(): held = lax.all_to_all(pieces, 'dp', split_axis=0, concat_axis=0, tiled=True)]
    reshape x4 -> x0, local copies, waits for them, and re-layouts: 8.07 us -> none  [the longest x1 4.24 us: shards(): down_t.reshape(owned, n_dp, rank * width // n_dp // 128, 128)]
    transpose x1 -> x0, local copies, waits for them, and re-layouts: 4.18 us -> none  [shards(): pieces = jnp.swapaxes(pieces, 0, 1)]
  transfers between devices with their start and end apart: 2 -> 0, of which waited for: 0 -> 0; matrix products, arithmetic and copies ran while one was open for 16% -> 0% of each run, Pallas kernels for 0% -> 0%
where the time goes in v2:
time: 83.7 us; the launch traced here: 83.6 us
  Pallas kernels  81.6 us (97%)
  local copies, waits for them, and re-layouts  1.31 us (2%)
    pallas_call x1, Pallas kernels, project(): pl.pallas_call(functools.partial(main_kernel, n_dp, n_t, k, upr), name=f'...  64.7 us
    pallas_call x1, Pallas kernels, gather_ids(): pl.pallas_call(functools.partial(ids_kernel, n_dp, owned, upr), name='gat...  17 us

profile of v2, /device:TPU:1, one launch (start us, length us, event | category | flops | bytes accessed | tf_op | source)
XLA Modules:
  0.0 83.6 jit_solution(12384913306818707302)
XLA Ops:
  0.0 17.0 %gather_ids.1 = (s32[8,256]{1,0:T(8,128)S(1)}, s32[256,128]{1,0:T(8,128)S(1)}) custom-call(s32[4]{0:T(128)} %ids_ref.1, s32[1,512]{1,0:T(1,128)} %bitcast.5), custom_call_target="tpu_custom_call" | custom-call | tf_op jit(solution)/shard_map/gather_ids/pallas_call | solution.py:360
  17.0 0.5 slice.3
  18.2 64.7 %conditional.1 = (bf16[2048,128]{1,0:T(8,128)(2,1)S(1)}) conditional(s32[]{:T(128)} %bitcast.1, (s32[8,256]{1,0:T(8,128)S(1)}, s32[256,128]{1,0:T(8,128)S(1)}, bf16[2048,1024]{1,0:T(8,128)(2,1)}, bf16[1024,1024]{1,0:T(8,128)(2,1)}, bf16[16,64,1024]{2,1,0:T(8,128)(2,1)}, /*index=5*/bf16[16,64,128]{2,1,0:T(8,128)(2,1)}) %tuple.16, ...), branch_computations={%region_0.0_spmd, %region_1.0_spmd} | conditional | bytes 8 | solution.py:457
  18.2 64.7 %project_6.1 = bf16[2048,128]{1,0:T(8,128)(2,1)S(1)} custom-call(s32[8,256]{1,0:T(8,128)S(1)} %get-tuple-element.38.row_ref, s32[256,128]{1,0:T(8,128)S(1)} %get-tuple-element.39.col_ref, bf16[2048,1024]{1,0:T(8,128)(2,1)} %get-tuple-element.56.tok_hbm, bf16[1024,1024]{1,0:T(8,128)(2,1)} %get-tuple-element.58.w_hbm, ...), custom_call_target="tpu_custom_call" | custom-call | tf_op jit(solution)/shard_map/cond/branch_1_fun/project_6/pallas_call | solution.py:390
  82.8 0.8 copy.18

commit v3 on v2

--- a/solution.py
+++ b/solution.py
@@ -24,7 +24,7 @@
     return half + (q % 2) * (n - 2 * half)
 
 
-def ids_kernel(n_dp, owned, upr, ids_ref, table_ref, row_ref, col_ref, mine, every, send_sem, recv_sem):
+def ids_kernel(n_dp, owned, upr, counts, ids_ref, table_ref, row_ref, col_ref, way_ref, mine, every, send_sem, recv_sem):
     dp = lax.axis_index("dp")
     shift = owned.bit_length() - 1
     rp = SLOTS * upr
@@ -38,11 +38,11 @@
     barrier = pltpu.get_barrier_semaphore()
 
     def greet(q, _):
-        peer = lax.rem(dp + q, n_dp)
+        peer = lax.rem(dp + visit(n_dp - 2 - q, n_dp), n_dp)
         pl.semaphore_signal(barrier, inc=1, device_id={"dp": peer}, device_id_type=MESH)
         return 0
 
-    lax.fori_loop(1, n_dp, greet, 0)
+    lax.fori_loop(0, n_dp - 1, greet, 0)
     pl.semaphore_wait(barrier, n_dp - 1)
 
     def push(step):
@@ -55,35 +55,38 @@
             device_id_type=MESH,
         )
 
-    def go(step, _):
-        push(step).start()
+    def go(q, _):
+        push(visit(n_dp - 2 - q, n_dp)).start()
         return 0
 
     def come(step, _):
         push(step).wait()
         return 0
 
-    lax.fori_loop(1, n_dp, go, 0)
+    lax.fori_loop(0, n_dp - 1, go, 0)
     lax.fori_loop(1, n_dp, come, 0)
 
     n = n_dp * rp
     ids = every[...].reshape(n, LANES)
     blocks = table_ref.shape[1] // LANES
     lane = iota((n, LANES), 1)
-    pos = jnp.zeros((n, 1), jnp.int32)
+    found = jnp.zeros((n, LANES), jnp.int32)
     for b in range(blocks):
         row = table_ref[:, b * LANES : (b + 1) * LANES]
         hit = ids == lane + b * LANES
-        pos += jnp.sum(jnp.where(hit, row, 0), axis=1, keepdims=True)
+        found += jnp.where(hit, row, 0)
+    pos = jnp.sum(found, axis=1, keepdims=True)
     owner = lax.shift_right_logical(pos, shift)
-    rank = jnp.zeros((n, 1), jnp.int32)
-    count = jnp.zeros((n, 1), jnp.int32)
+    before = jnp.zeros((n, LANES), jnp.int32)
+    among = jnp.zeros((n, LANES), jnp.int32)
     for b in range(blocks):
         at = lane + b * LANES
         needed = jnp.max(jnp.where(pos == at, 1, 0), axis=0, keepdims=True)
         same = jnp.where(lax.shift_right_logical(at, shift) == owner, needed, 0)
-        count += jnp.sum(same, axis=1, keepdims=True)
-        rank += jnp.sum(jnp.where(at < pos, same, 0), axis=1, keepdims=True)
+        among += same
+        before += jnp.where(at < pos, same, 0)
+    count = jnp.sum(among, axis=1, keepdims=True)
+    rank = jnp.sum(before, axis=1, keepdims=True)
     code = owner * owned + rank
     col_ref[...] = jnp.broadcast_to(code, (n, LANES))
     for b in range(n // LANES):
@@ -91,15 +94,16 @@
         row_ref[0:1, b * LANES : (b + 1) * LANES] = jnp.sum(jnp.where(diag, code, 0), axis=0, keepdims=True)
     own = jnp.where((owner == dp) & (rank == lane), pos - dp * owned, 0)
     row_ref[1:2, 0:LANES] = jnp.max(own, axis=0, keepdims=True)
-    row_ref[2:3, 0:LANES] = jnp.broadcast_to(jnp.max(count, axis=0, keepdims=True), (1, LANES))
+    most = jnp.max(count, axis=0, keepdims=True)
+    way_ref[...] = sum(jnp.where(most > c, 1, 0) for c in counts[:-1])
 
 
 def main_kernel(
     n_dp, n_t, k, upr,
     row_ref, col_ref, tok_hbm, w_hbm, down_hbm, up_hbm, out_ref,
     tok, w, down, up, upt, stage, held, outb, land, part, pair, anti, fwd, bwd, hop_a, hop_b, got_f, got_b,
-    panel, lowp, lowr, lowb, lowa,
-    load_sem, s1, r1, s2, r2, sp, rp_, sh, rh, s3, r3, s4, r4,
+    panel, lown, lowp, lowr, lowb, lowa,
+    load_sem, s1, r1, s2, r2, s5, r5, sp, rp_, sh, rh, s3, r3, s4, r4,
 ):
     dp = lax.axis_index("dp")
     t = lax.axis_index("tensor")
@@ -115,7 +119,7 @@
     no = SLOTS + nuo
     rp = SLOTS * upr
     half = n_rows // 2
-    tb = n_rows // n_t
+    tb = n_rows // (2 * n_t)
 
     loads = [
         pltpu.make_async_copy(a, b, load_sem.at[i])
@@ -137,6 +141,11 @@
     lax.fori_loop(1, n_dp, greet_dp, 0)
     lax.fori_loop(1, n_t, greet_t, 0)
 
+    kk = nu * ROWS // upr
+    m = n_dp * nu * ROWS
+    r = iota((m, 1), 0)
+    src = (r % (nu * ROWS)) // upr * rank + r // (nu * ROWS) * upr + r % upr
+    perm = jnp.where(src == iota((m, kk * rank), 1), 1.0, 0.0).astype(jnp.bfloat16)
     loads[0].wait()
     loads[1].wait()
 
@@ -148,13 +157,8 @@
         return 0
 
     lax.fori_loop(0, k, pick, 0)
-    kk = nu * ROWS // upr
     for j in range(kk):
         upt[j * rank : (j + 1) * rank, :] = up[row_ref[1, min(j, k - 1)]]
-    m = n_dp * nu * ROWS
-    r = iota((m, kk * rank), 0)
-    src = (r % (nu * ROWS)) // upr * rank + r // (nu * ROWS) * upr + r % upr
-    perm = jnp.where(src == iota((m, kk * rank), 1), 1.0, 0.0).astype(jnp.bfloat16)
     ups = jnp.dot(perm, upt[0 : kk * rank, :], preferred_element_type=jnp.float32).astype(jnp.bfloat16)
     for i in range(n_dp):
         for u in range(nu):
@@ -163,11 +167,11 @@
 
     pl.semaphore_wait(barrier, n_dp - 1 + n_t - 1)
 
-    def exchange(src_ref, dst_ref, size, send_sem, recv_sem, step):
+    def exchange(src_ref, dst_ref, size, at, amount, send_sem, recv_sem, step):
         peer = lax.rem(dp + step, n_dp)
         return pltpu.make_async_remote_copy(
-            src_ref=src_ref.at[pl.ds(peer * size, size)],
-            dst_ref=dst_ref.at[pl.ds(dp * size, size)],
+            src_ref=src_ref.at[pl.ds(peer * size + at, amount)],
+            dst_ref=dst_ref.at[pl.ds(dp * size + at, amount)],
             send_sem=send_sem.at[step],
             recv_sem=recv_sem.at[step],
             device_id={"dp": peer},
@@ -189,8 +193,12 @@
 
         lax.fori_loop(0, n_dp - 1, body, 0)
 
-    first = functools.partial(exchange, stage, held, nt, s1, r1)
-    second = functools.partial(exchange, outb, land, no, s2, r2)
+    first = functools.partial(exchange, stage, held, nt, 0, nt, s1, r1)
+    early = SLOTS // 2
+    second = [
+        functools.partial(exchange, outb, land, no, 0, early, s2, r2),
+        functools.partial(exchange, outb, land, no, early, no - early, s5, r5),
+    ]
 
     start_all(first)
 
@@ -258,22 +266,30 @@
     bwd[hi, :] = (both(3, hi) + hop_b[...].astype(jnp.float32)).astype(jnp.bfloat16)
     bwd_hi.start()
 
-    wait_all(first, "recv")
-
-    def serve(d, _):
-        for s in range(SLOTS):
-            code = row_ref[0, d * rp + s * upr]
-            outb[d * no + s] = held[lax.div(code, owned) * nt + lax.rem(code, owned)]
-        return 0
-
-    lax.fori_loop(0, n_dp, serve, 0)
-    source = jnp.concatenate([held[o * nt + k + u] for o in range(n_dp) for u in range(nu)], axis=0)
     shape = (n_dp * rp, n_dp * nu * ROWS)
     code = col_ref[:, 0:1]
     shift = owned.bit_length() - 1
     src = lax.shift_right_logical(code, shift) * (nu * ROWS) + (code & (owned - 1)) * upr
     src = src + iota((n_dp * rp, 1), 0) % upr
     pickup = jnp.where(src == iota(shape, 1), 1.0, 0.0).astype(jnp.bfloat16)
+    r = iota((SLOTS * rank, 1), 0)
+    src = (r % rank) // upr * (nuo * ROWS) + r // rank * upr + r % upr
+    arrange = jnp.where(src == iota((SLOTS * rank, n_dp * nuo * ROWS), 1), 1.0, 0.0).astype(jnp.bfloat16)
+    wait_all(first, "recv")
+
+    def serve(slots):
+        def body(d, _):
+            for s in slots:
+                code = row_ref[0, d * rp + s * upr]
+                outb[d * no + s] = held[lax.shift_right_logical(code, shift) * nt + (code & (owned - 1))]
+            return 0
+
+        lax.fori_loop(0, n_dp, body, 0, unroll=4)
+
+    serve(range(early))
+    start_all(second[0])
+    serve(range(early, SLOTS))
+    source = jnp.concatenate([held[o * nt + k + u] for o in range(n_dp) for u in range(nu)], axis=0)
     ups = jnp.dot(pickup, source, preferred_element_type=jnp.float32).reshape(n_dp, rp, LANES)
     if rp < nuo * ROWS:
         ups = jnp.concatenate([ups, jnp.zeros((n_dp, nuo * ROWS - rp, LANES), jnp.float32)], axis=1)
@@ -281,91 +297,101 @@
     for d in range(n_dp):
         for u in range(nuo):
             outb[d * no + SLOTS + u] = ups[d, u * ROWS : (u + 1) * ROWS, :]
-    start_all(second)
+    start_all(second[1])
 
     def keep2(b, _):
         land[dp * no + b] = outb[dp * no + b]
         return 0
 
     lax.fori_loop(0, no, keep2, 0)
-    wait_all(second, "recv")
-
-    for i in range(n_dp):
-        rg, cg = divmod(i, ncg)
-        for s in range(SLOTS):
-            panel[s, rg * ROWS : (rg + 1) * ROWS, cg * LANES : (cg + 1) * LANES] = land[i * no + s]
-
-    per = n_t // SLOTS
-    for s in range(SLOTS):
-        low = lax.dot_general(
-            panel[s], tok[s * seq : (s + 1) * seq, :], (((1,), (1,)), ((), ())),
-            preferred_element_type=jnp.float32,
-        )
-        for h in range(per):
-            lowp[s * per + h] = low[:, h * tb : (h + 1) * tb]
-
-    def spread(src, dst, send_sem, recv_sem, step, by_peer):
+
+    def spread(src, dst, send_sem, recv_sem, g, step, by_peer):
         peer = lax.rem(t + step, n_t)
         return to_tensor(
-            src.at[peer] if by_peer else src, dst.at[t], send_sem.at[step], recv_sem.at[step], peer
+            src.at[g, peer] if by_peer else src.at[g], dst.at[g, t], send_sem.at[g, step], recv_sem.at[g, step], peer
         )
 
-    scatter = [spread(lowp, lowr, s3, r3, q, True) for q in range(1, n_t)]
-    for cp in scatter:
-        cp.start()
-    lowr[t] = lowp[t]
+    scatter = [[spread(lowp, lowr, s3, r3, g, q, True) for q in range(1, n_t)] for g in range(2)]
+    gather = [[spread(lowb, lowa, s4, r4, g, q, False) for q in range(1, n_t)] for g in range(2)]
+    per = n_t // early
+
+    def low_part(g):
+        for s in range(g * early, (g + 1) * early):
+            for i in range(n_dp):
+                rg, cg = divmod(i, ncg)
+                panel[s, rg * ROWS : (rg + 1) * ROWS, cg * LANES : (cg + 1) * LANES] = land[i * no + s]
+            low = lax.dot_general(
+                panel[s], tok[s * seq : (s + 1) * seq, :], (((1,), (1,)), ((), ())),
+                preferred_element_type=jnp.float32,
+            )
+            for h in range(per):
+                b = (s - g * early) * per + h
+                lown[g, b] = low[:, h * tb : (h + 1) * tb]
+                lowp[g, b] = low[:, h * tb : (h + 1) * tb].astype(jnp.bfloat16)
+        for cp in scatter[g]:
+            cp.start()
+
+    def low_total(g):
+        for cp in scatter[g]:
+            cp.wait_recv()
+        total = lown[g, t]
+        for q in range(1, n_t):
+            total = total + lowr[g, lax.rem(t + q, n_t)].astype(jnp.float32)
+        lowb[g] = total.astype(jnp.bfloat16)
+        for cp in gather[g]:
+            cp.start()
+        lowa[g, t] = total.astype(jnp.bfloat16)
+
+    def finish(g):
+        for cp in gather[g]:
+            cp.wait_recv()
+        for b in range(n_t):
+            s = g * early + b // per
+            rows = pl.ds((g * n_t + b) * tb, tb)
+            delta = lax.dot_general(
+                lowa[g, b], ups[s * rank : (s + 1) * rank, :], (((0,), (0,)), ((), ())),
+                preferred_element_type=jnp.float32,
+            )
+            base = both(0, rows) + got_f[rows, :].astype(jnp.float32) + got_b[rows, :].astype(jnp.float32)
+            out_ref[rows, :] = (base + adapter_scale * delta).astype(jnp.bfloat16)
+
+    wait_all(second[0], "recv")
+    low_part(0)
+    low_total(0)
+    wait_all(second[1], "recv")
+    low_part(1)
     source = jnp.concatenate([land[i * no + SLOTS + u] for i in range(n_dp) for u in range(nuo)], axis=0)
-    shape = (SLOTS * rank, n_dp * nuo * ROWS)
-    r = iota(shape, 0)
-    src = (r % rank) // upr * (nuo * ROWS) + r // rank * upr + r % upr
-    perm = jnp.where(src == iota(shape, 1), 1.0, 0.0).astype(jnp.bfloat16)
-    ups = jnp.dot(perm, source, preferred_element_type=jnp.float32).astype(jnp.bfloat16)
-    for cp in scatter:
-        cp.wait_recv()
-    total = lowr[0]
-    for q in range(1, n_t):
-        total = total + lowr[q]
-    lowb[...] = total.astype(jnp.bfloat16)
-    gather = [spread(lowb, lowa, s4, r4, q, False) for q in range(1, n_t)]
-    for cp in gather:
-        cp.start()
-    lowa[t] = total.astype(jnp.bfloat16)
-
+    ups = jnp.dot(arrange, source, preferred_element_type=jnp.float32).astype(jnp.bfloat16)
     pairs[0].wait_recv()
     fwd_hi.wait_recv()
     bwd_lo.wait_recv()
     fwd_lo.wait_recv()
     bwd_hi.wait_recv()
-    for cp in gather:
-        cp.wait_recv()
-    for b in range(n_t):
-        rows = pl.ds(b * tb, tb)
-        delta = lax.dot_general(
-            lowa[b], ups[b // per * rank : (b // per + 1) * rank, :], (((0,), (0,)), ((), ())),
-            preferred_element_type=jnp.float32,
-        )
-        base = both(0, rows) + got_f[rows, :].astype(jnp.float32) + got_b[rows, :].astype(jnp.float32)
-        out_ref[rows, :] = (base + adapter_scale * delta).astype(jnp.bfloat16)
+    finish(0)
+    low_total(1)
+    finish(1)
 
     wait_all(first, "send")
-    wait_all(second, "send")
+    for part_of in second:
+        wait_all(part_of, "send")
     for rel in range(4):
         pairs[rel].wait_send()
-    for cp in (send_a, send_b, fwd_hi, bwd_lo, fwd_lo, bwd_hi, *scatter, *gather):
+    for cp in (send_a, send_b, fwd_hi, bwd_lo, fwd_lo, bwd_hi, *scatter[0], *scatter[1], *gather[0], *gather[1]):
         cp.wait_send()
 
 
-def gather_ids(n_dp, owned, upr, ids, table):
+def gather_ids(n_dp, owned, upr, counts, ids, table):
     n = n_dp * SLOTS * upr
     return pl.pallas_call(
-        functools.partial(ids_kernel, n_dp, owned, upr),
+        functools.partial(ids_kernel, n_dp, owned, upr, counts),
         name="gather_ids",
         out_shape=(
             jax.ShapeDtypeStruct((8, n), jnp.int32),
             jax.ShapeDtypeStruct((n, LANES), jnp.int32),
+            jax.ShapeDtypeStruct((1, 1), jnp.int32),
         ),
         in_specs=[pl.BlockSpec(memory_space=pltpu.SMEM), pl.BlockSpec(memory_space=pltpu.VMEM)],
-        out_specs=(pl.BlockSpec(memory_space=pltpu.VMEM), pl.BlockSpec(memory_space=pltpu.VMEM)),
+        out_specs=(pl.BlockSpec(memory_space=pltpu.VMEM),) * 3,
         scratch_shapes=[
             pltpu.VMEM((SLOTS * upr, LANES), jnp.int32),
             pltpu.VMEM((n_dp, SLOTS * upr, LANES), jnp.int32),
@@ -385,7 +411,7 @@
     kk = -(-upr * k // ROWS) * ROWS // upr
     bf, f32 = jnp.bfloat16, jnp.float32
     dma = pltpu.SemaphoreType.DMA
-    half, tb = n_rows // 2, n_rows // n_t
+    half, tb = n_rows // 2, n_rows // (2 * n_t)
     anywhere = pl.BlockSpec(memory_space=pl.ANY)
     return pl.pallas_call(
         functools.partial(main_kernel, n_dp, n_t, k, upr),
@@ -417,17 +443,19 @@
             pltpu.VMEM((n_rows, LANES), bf),
             pltpu.VMEM((n_rows, LANES), bf),
             pltpu.VMEM((SLOTS, rank, width), bf),
-            pltpu.VMEM((n_t, rank, tb), f32),
-            pltpu.VMEM((n_t, rank, tb), f32),
-            pltpu.VMEM((rank, tb), bf),
-            pltpu.VMEM((n_t, rank, tb), bf),
+            pltpu.VMEM((2, n_t, rank, tb), f32),
+            pltpu.VMEM((2, n_t, rank, tb), bf),
+            pltpu.VMEM((2, n_t, rank, tb), bf),
+            pltpu.VMEM((2, rank, tb), bf),
+            pltpu.VMEM((2, n_t, rank, tb), bf),
             dma((4,)),
+            dma((n_dp,)), dma((n_dp,)),
             dma((n_dp,)), dma((n_dp,)),
             dma((n_dp,)), dma((n_dp,)),
             dma((4,)), dma((4,)),
             dma((6,)), dma((6,)),
-            dma((n_t,)), dma((n_t,)),
-            dma((n_t,)), dma((n_t,)),
+            dma((2, n_t)), dma((2, n_t)),
+            dma((2, n_t)), dma((2, n_t)),
         ],
         compiler_params=pltpu.CompilerParams(
             collective_id=collective_id, has_side_effects=True, vmem_limit_bytes=VMEM_LIMIT
@@ -435,7 +463,7 @@
     )(rows_info, cols_info, tokens, weight, down_t, up)
 
 
-FEW = 6
+COUNTS = (4, 5, 6, 8)
 
 
 def shards(
@@ -450,14 +478,14 @@
     owned, width, rank = adapter_down_weight.shape
     upr = rank // n_dp
     down_t = jnp.swapaxes(adapter_down_weight, 1, 2)
-    rows_info, cols_info = gather_ids(
-        n_dp, owned, upr, request_adapter_index, storage_index_table.reshape(1, -1)
+    counts = (*(c for c in COUNTS if c < owned), owned)
+    rows_info, cols_info, way = gather_ids(
+        n_dp, owned, upr, counts, request_adapter_index, storage_index_table.reshape(1, -1)
     )
     operands = (rows_info, cols_info, tokens, base_value_weight, down_t, adapter_up_weight)
-    return lax.cond(
-        rows_info[2, 0] <= FEW,
-        functools.partial(project, n_dp, n_t, FEW, upr, 1),
-        functools.partial(project, n_dp, n_t, owned, upr, 2),
+    return lax.switch(
+        way[0, 0],
+        [functools.partial(project, n_dp, n_t, c, upr, 1 + i) for i, c in enumerate(counts)],
         *operands,
     )
 

time: 83.7 us -> 77.2 us (0.922)
  Pallas kernels: 81.6 us -> 75.4 us
    pallas_call x1, Pallas kernels: 64.7 us -> 58.8 us  [project(): pl.pallas_call(functools.partial(main_kernel, n_dp, n_t, k, upr), name=f'...]
where the time goes in v3:
time: 77.2 us; the launch traced here: 77.1 us
  Pallas kernels  75.4 us (98%)
  local copies, waits for them, and re-layouts  0.8 us (1%)
    pallas_call x1, Pallas kernels, project(): pl.pallas_call(functools.partial(main_kernel, n_dp, n_t, k, upr), name=f'...  58.8 us
    pallas_call x1, Pallas kernels, gather_ids(): pl.pallas_call(functools.partial(ids_kernel, n_dp, owned, upr, counts), n...  16.6 us

profile of v3, /device:TPU:1, one launch (start us, length us, event | category | flops | bytes accessed | tf_op | source)
XLA Modules:
  0.0 77.1 jit_solution(3507259833324344324)
XLA Ops:
  0.0 16.6 %gather_ids.1 = (s32[8,256]{1,0:T(8,128)S(1)}, s32[256,128]{1,0:T(8,128)S(1)}, s32[1,1]{1,0:T(1,128)}) custom-call(s32[4]{0:T(128)} %ids_ref.1, s32[1,512]{1,0:T(1,128)} %bitcast.8), custom_call_target="tpu_custom_call" | custom-call | tf_op jit(solution)/shard_map/gather_ids/pallas_call | solution.py:385
  17.3 59.0 %conditional.1 = (bf16[2048,128]{1,0:T(8,128)(2,1)S(1)}) conditional(s32[]{:T(128)} %bitcast.1, (s32[8,256]{1,0:T(8,128)S(1)}, s32[256,128]{1,0:T(8,128)S(1)}, bf16[2048,1024]{1,0:T(8,128)(2,1)}, bf16[1024,1024]{1,0:T(8,128)(2,1)}, bf16[16,64,1024]{2,1,0:T(8,128)(2,1)}, ...), branch_computations={%region_0.0_spmd, %region_1.0_spmd, %region_2.0_spmd, %region_3.0_... | conditional | bytes 8 | solution.py:486
  17.3 58.8 %project_5.1 = bf16[2048,128]{1,0:T(8,128)(2,1)S(1)} custom-call(s32[8,256]{1,0:T(8,128)S(1)} %get-tuple-element.77.row_ref, s32[256,128]{1,0:T(8,128)S(1)} %get-tuple-element.78.col_ref, bf16[2048,1024]{1,0:T(8,128)(2,1)} %get-tuple-element.124.tok_hbm, bf16[1024,1024]{1,0:T(8,128)(2,1)} %get-tuple-element.129.w_hbm, ...), custom_call_target="tpu_custom_call" | custom-call | tf_op jit(solution)/shard_map/cond/branch_1_fun/project_5/pallas_call | solution.py:416
  76.3 0.8 %copy.33 = bf16[2048,128]{1,0:T(8,128)(2,1)} copy(bf16[2048,128]{1,0:T(8,128)(2,1)S(1)} %get-tuple-element.107) | data formatting | bytes 1048576
